TPU v7x, 32 devices: a whole 2x2x4 slice. The times are simulated.
32 devices in a mesh: gx: 8 (over z, x), gy: 4 (over y, core).
Axes of the slice: x: 2, y: 2, z: 4, core: 2. Of those that a mesh axis runs over, the one named last changes fastest.
Arguments:
- velocity: float32 [3, 1, 1024, 2560], P(None, None, 'gy', 'gx'), may hold values from -12 to 12
- grid_x: float32 [33], replicated, may hold values from 0.05 to 1
- grid_y: float32 [1024, 33], P('gy'), may hold values from 0.05 to 1
- test_x: float32 [33], replicated, may hold values from 0.05 to 1
- test_y: float32 [1024, 33], P('gy'), may hold values from 0.05 to 1
Outputs:
- subgrid: float32 [6, 1, 1024, 2560], P(None, None, 'gy', 'gx')
- germano: float32 [6, 1, 1024, 2560], P(None, None, 'gy', 'gx')
All inputs are finite; a program needn't handle non-finite values.
Results may differ from a plain program's by a relative error of at most 0.0001.
Values sent between devices are 32-bit elements; how exact they have to be, the bound alone decides.
A program may use at most 64 MiB of HBM per device.

v0:
```python
import functools

import jax
import jax.numpy as jnp
from jax import lax
from jax.experimental import pallas as pl
from jax.experimental.pallas import tpu as pltpu
from jax.sharding import PartitionSpec as P

MESH = pl.DeviceIdType.MESH
LANES = 128
SUB = 8
DIRECTIONS = [(1, 0), (-1, 0), (0, 1), (0, -1), (1, 1), (-1, 1), (1, -1), (-1, -1)]
BF = jnp.bfloat16
F32 = jnp.float32


def round_up(value, unit):
    return (value + unit - 1) // unit * unit


def halo_kernel(nx, ny, width, v_ref, t_ref, ext_ref, text_ref,
                pack_l, pack_r, from_l, from_r, from_d, from_u, corners, t_low, t_high,
                send_sem, recv_sem):
    comps, rows, cols = v_ref.shape
    margin = t_low.shape[0]
    me_x, me_y = lax.axis_index("gx"), lax.axis_index("gy")

    def device(dx, dy):
        return {"gx": lax.rem(me_x + dx + nx, nx), "gy": lax.rem(me_y + dy + ny, ny)}

    barrier = pltpu.get_barrier_semaphore()
    for dx, dy in DIRECTIONS:
        pl.semaphore_signal(barrier, inc=1, device_id=device(dx, dy), device_id_type=MESH)

    per = LANES // width
    groups = rows // width
    for c in range(comps):
        for g in range(groups):
            for q in range(per):
                src = pl.ds(g * width + q * SUB, SUB)
                dst = pl.ds(g * SUB, SUB)
                pack_r[c, dst, q * width:(q + 1) * width] = v_ref[c, src, cols - width:cols]
                pack_l[c, dst, q * width:(q + 1) * width] = v_ref[c, src, 0:width]
    pl.semaphore_wait(barrier, len(DIRECTIONS))

    top = pl.ds((groups - 1) * SUB, SUB)
    low = pl.ds(0, SUB)
    sources = [
        pack_r, pack_l,
        v_ref.at[:, pl.ds(rows - width, width), :], v_ref.at[:, pl.ds(0, width), :],
        pack_r.at[:, top, :], pack_l.at[:, top, :], pack_r.at[:, low, :], pack_l.at[:, low, :],
    ]
    targets = [from_l, from_r, from_d, from_u] + [corners.at[i] for i in range(4)]
    copies = []
    for i, (dx, dy) in enumerate(DIRECTIONS):
        copies.append((dy, pltpu.make_async_remote_copy(
            src_ref=sources[i], dst_ref=targets[i], send_sem=send_sem.at[i],
            recv_sem=recv_sem.at[i], device_id=device(dx, dy), device_id_type=MESH)))
    for i, (dy, src, dst) in enumerate([
        (1, t_ref.at[pl.ds(rows - margin, margin), :], t_low),
        (-1, t_ref.at[pl.ds(0, margin), :], t_high),
    ]):
        n = len(DIRECTIONS) + i
        copies.append((dy, pltpu.make_async_remote_copy(
            src_ref=src, dst_ref=dst, send_sem=send_sem.at[n],
            recv_sem=recv_sem.at[n], device_id=device(0, dy), device_id_type=MESH)))

    has_up, has_down = me_y < ny - 1, me_y > 0
    for dy, copy in copies:
        if dy == 0:
            copy.start()
    for sign, present in ((1, has_up), (-1, has_down)):
        @pl.when(present)
        def _(sign=sign):
            for dy, copy in copies:
                if dy == sign:
                    copy.start()

    wide = ext_ref.shape[2]
    high = rows + width
    for c in range(comps):
        ext_ref[c, pl.ds(width, rows), width:width + cols] = v_ref[c]
    if wide > cols + 2 * width:
        ext_ref[:, :, cols + 2 * width:] = jnp.zeros(
            (comps, rows + 2 * width, wide - cols - 2 * width), F32)
    text_ref[...] = jnp.zeros_like(text_ref)
    text_ref[pl.ds(margin, rows), 0:t_ref.shape[1]] = t_ref[...]

    def unpack(buf, c, row, lane, count):
        for g in range(count):
            for q in range(per):
                ext_ref[c, pl.ds(row + g * width + q * SUB, SUB), lane:lane + width] = (
                    buf[c, pl.ds(g * SUB, SUB), q * width:(q + 1) * width])

    for sign, present, row, mid, pair, taps, trow in (
        (1, has_down, 0, from_d, (0, 1), t_low, 0),
        (-1, has_up, high, from_u, (2, 3), t_high, margin + rows),
    ):
        @pl.when(present)
        def _(sign=sign, row=row, mid=mid, pair=pair, taps=taps, trow=trow):
            for dy, copy in copies:
                if dy == sign:
                    copy.wait_recv()
            for c in range(comps):
                ext_ref[c, pl.ds(row, width), width:width + cols] = mid[c]
                unpack(corners.at[pair[0]], c, row, 0, 1)
                unpack(corners.at[pair[1]], c, row, width + cols, 1)
            text_ref[pl.ds(trow, margin), 0:t_ref.shape[1]] = taps[...]

        @pl.when(jnp.logical_not(present))
        def _(row=row):
            for c in range(comps):
                ext_ref[c, pl.ds(row, width), :] = jnp.zeros((width, wide), F32)

    copies[0][1].wait_recv()
    for c in range(comps):
        unpack(from_l, c, width, 0, groups)
    copies[1][1].wait_recv()
    for c in range(comps):
        unpack(from_r, c, width, width + cols, groups)

    for dy, copy in copies:
        if dy == 0:
            copy.wait_send()
    for sign, present in ((1, has_up), (-1, has_down)):
        @pl.when(present)
        def _(sign=sign):
            for dy, copy in copies:
                if dy == sign:
                    copy.wait_send()


def split(value):
    high = value.astype(BF)
    return high, (value - high.astype(F32)).astype(BF)


def pair_of(p):
    first = jnp.where(p < 3, 0, jnp.where(p < 5, 1, 2))
    second = jnp.where(p < 3, p, jnp.where(p < 5, p - 2, 2))
    return first, second


def stress_kernel(ny, taps, ext_ref, text_ref, gx_ref, tx_ref, ty_ref, sub_ref, ger_ref,
                  inner, coarse, coarse_in, tested, gxb, txb, gyb, gib, tyb, zh, zl):
    comps = ext_ref.shape[0]
    rows, cols = sub_ref.shape[1], sub_ref.shape[2]
    wide = ext_ref.shape[2]
    margin = (taps - 1) // 2
    rows_mid = rows + 2 * margin
    rows_ext = rows + 4 * margin
    first_row = lax.axis_index("gy") * rows
    total = rows * ny
    blk = LANES
    lane_tiles = wide // blk

    def skew(table):
        return pltpu.roll(table, 0, 1, stride=1, stride_axis=0)

    lane = lax.broadcasted_iota(jnp.int32, (blk, 2 * blk), 1)

    def x_band(w_ref, out):
        w = jnp.concatenate([w_ref[...], jnp.zeros((1, 2 * blk - w_ref.shape[1]), F32)], axis=1)
        w = w / jnp.sum(w)
        high, low = split(skew(jnp.broadcast_to(w, (blk, 2 * blk))))
        out[0], out[1] = high, low

    x_band(gx_ref, gxb)
    x_band(tx_ref, txb)

    def y_bands(load, row0, count, out):
        for n, start in enumerate(range(0, count, blk)):
            size = min(blk, count - start)
            raw = load(start, size)
            raw = jnp.concatenate([raw, jnp.zeros((size, 2 * blk - raw.shape[1]), F32)], axis=1)
            k = lax.broadcasted_iota(jnp.int32, (size, 2 * blk), 1)
            y = row0 + start + lax.broadcasted_iota(jnp.int32, (size, 2 * blk), 0)
            source = y + k - margin
            keep = (k < taps) & (source >= 0) & (source < total) & (y >= 0) & (y < total)
            w = jnp.where(keep, raw, 0.0)
            s = jnp.sum(w, axis=1, keepdims=True)
            w = w / jnp.where(s > 0.0, s, 1.0)
            high, low = split(skew(w))
            out[n, 0, 0:size], out[n, 1, 0:size] = high, low

    y_bands(lambda a, n: text_ref[pl.ds(a, n), :], first_row - margin, rows_mid, gyb)
    y_bands(lambda a, n: text_ref[pl.ds(a + margin, n), :], first_row, rows, gib)
    y_bands(lambda a, n: ty_ref[pl.ds(a, n), :], first_row, rows, tyb)

    def dot_t(a, b):
        return lax.dot_general(a, b, (((1,), (1,)), ((), ())), preferred_element_type=F32)

    def dot(a, b):
        return jnp.dot(a, b, preferred_element_type=F32)

    def filtered(load, rows_in, xb, yb, put):
        rows_out = rows_in - 2 * margin
        high, low = split(load())
        for t in range(lane_tiles):
            k0, k1 = t * blk, min((t + 2) * blk, wide)
            bh, bl = xb[0, :, 0:k1 - k0], xb[1, :, 0:k1 - k0]
            z = dot_t(high[:, k0:k1], bh) + dot_t(high[:, k0:k1], bl) + dot_t(low[:, k0:k1], bh)
            h, l = split(z)
            zh[0:rows_in, k0:k0 + blk] = h
            zl[0:rows_in, k0:k0 + blk] = l
        for n, start in enumerate(range(0, rows_out, blk)):
            size = min(blk, rows_out - start)
            k = size + 2 * margin
            bh, bl = yb[n, 0, 0:size, 0:k], yb[n, 1, 0:size, 0:k]
            dh, dl = zh[start:start + k, :], zl[start:start + k, :]
            put(start, size, dot(bh, dh) + dot(bl, dh) + dot(bh, dl))

    @pl.loop(0, comps)
    def _(c):
        inner[c] = pltpu.roll(ext_ref[c, pl.ds(margin, rows_mid), :], wide - margin, 1)

        def put(start, size, value):
            coarse[c, pl.ds(start, size), :] = value

        filtered(lambda: ext_ref[c], rows_ext, gxb, gyb, put)
        coarse_in[c] = pltpu.roll(coarse[c, pl.ds(margin, rows), :], wide - margin, 1)

        def put_tested(start, size, value):
            tested[c, pl.ds(start, size), :] = value

        filtered(lambda: coarse[c], rows_mid, txb, tyb, put_tested)

    @pl.loop(0, sub_ref.shape[0])
    def _(p):
        i, j = pair_of(p)

        def put_sub(start, size, value):
            at = pl.ds(start, size)
            sub_ref[p, at, :] = (value - coarse_in[i, at, :] * coarse_in[j, at, :])[:, 0:cols]

        filtered(lambda: inner[i] * inner[j], rows_mid, gxb, gib, put_sub)

        def put_ger(start, size, value):
            at = pl.ds(start, size)
            ger_ref[p, at, :] = (value - tested[i, at, :] * tested[j, at, :])[:, 0:cols]

        filtered(lambda: coarse[i] * coarse[j], rows_mid, txb, tyb, put_ger)


def local(nx, ny, velocity, grid_x, grid_y, test_x, test_y):
    comps, planes, rows, cols = velocity.shape
    taps = grid_x.shape[0]
    margin = (taps - 1) // 2
    width = 2 * margin
    wide = round_up(cols + 2 * width, LANES)
    pairs = comps * (comps + 1) // 2
    vmem = pl.BlockSpec(memory_space=pltpu.VMEM)
    packed = rows // width * SUB
    subs, gers = [], []
    rows_mid, rows_ext = rows + width, rows + 2 * width
    for plane in range(planes):
        v = velocity[:, plane]
        ext, text = pl.pallas_call(
            functools.partial(halo_kernel, nx, ny, width),
            out_shape=(
                jax.ShapeDtypeStruct((comps, rows_ext, wide), F32),
                jax.ShapeDtypeStruct((rows_mid, LANES), F32),
            ),
            in_specs=[vmem] * 2,
            out_specs=(vmem, vmem),
            scratch_shapes=[
                pltpu.VMEM((comps, packed, LANES), F32),
                pltpu.VMEM((comps, packed, LANES), F32),
                pltpu.VMEM((comps, packed, LANES), F32),
                pltpu.VMEM((comps, packed, LANES), F32),
                pltpu.VMEM((comps, width, cols), F32),
                pltpu.VMEM((comps, width, cols), F32),
                pltpu.VMEM((4, comps, SUB, LANES), F32),
                pltpu.VMEM((margin, taps), F32),
                pltpu.VMEM((margin, taps), F32),
                pltpu.SemaphoreType.DMA((len(DIRECTIONS) + 2,)),
                pltpu.SemaphoreType.DMA((len(DIRECTIONS) + 2,)),
            ],
            compiler_params=pltpu.CompilerParams(
                collective_id=plane, has_side_effects=True, vmem_limit_bytes=16 << 20),
            name="halo",
        )(v, grid_y)
        out = jax.ShapeDtypeStruct((pairs, rows, cols), F32)
        tiles_mid, tiles = pl.cdiv(rows_mid, LANES), pl.cdiv(rows, LANES)
        sub, ger = pl.pallas_call(
            functools.partial(stress_kernel, ny, taps),
            out_shape=(out, out),
            in_specs=[vmem] * 5,
            out_specs=(vmem, vmem),
            scratch_shapes=[
                pltpu.VMEM((comps, rows_mid, wide), F32),
                pltpu.VMEM((comps, rows_mid, wide), F32),
                pltpu.VMEM((comps, rows, wide), F32),
                pltpu.VMEM((comps, rows, wide), F32),
                pltpu.VMEM((2, LANES, 2 * LANES), BF),
                pltpu.VMEM((2, LANES, 2 * LANES), BF),
                pltpu.VMEM((tiles_mid, 2, LANES, 2 * LANES), BF),
                pltpu.VMEM((tiles, 2, LANES, 2 * LANES), BF),
                pltpu.VMEM((tiles, 2, LANES, 2 * LANES), BF),
                pltpu.VMEM((rows_ext, wide), BF),
                pltpu.VMEM((rows_ext, wide), BF),
            ],
            compiler_params=pltpu.CompilerParams(vmem_limit_bytes=40 << 20),
            name="stress",
        )(ext, text, grid_x.reshape(1, taps), test_x.reshape(1, taps), test_y)
        subs.append(sub)
        gers.append(ger)
    return jnp.stack(subs, axis=1), jnp.stack(gers, axis=1)


def solution(mesh):
    nx, ny = mesh.shape["gx"], mesh.shape["gy"]
    field = P(None, None, "gy", "gx")
    return jax.shard_map(
        functools.partial(local, nx, ny),
        mesh=mesh,
        in_specs=(field, P(), P("gy", None), P(), P("gy", None)),
        out_specs=(field, field),
        check_vma=False,
    )
```

profile of v0, /device:TPU:0, one launch (start us, length us, event | category | flops | bytes accessed | tf_op | source)
XLA Modules:
  0.0 37.5 jit_solution(17030753380855301298)
XLA Ops:
  0.6 0.0 copy-start.2
  0.6 0.0 copy-start.1
  0.7 0.9 %copy.8.t_ref = f32[256,33]{1,0:T(8,128)S(1)} copy(f32[256,33]{0,1:T(8,128)} %param.7) | data formatting | bytes 67584 | tf_op args[2]
  1.5 0.9 %copy.9.ty_ref = f32[256,33]{1,0:T(8,128)S(1)} copy(f32[256,33]{0,1:T(8,128)} %param.9) | data formatting | bytes 67584 | tf_op args[4]
  2.4 1.6 %copy.7 = f32[3,1,256,320]{3,2,0,1:T(8,128)S(1)} copy(f32[3,1,256,320]{2,3,1,0:T(8,128)} %param.5) | data formatting | bytes 1966080 | tf_op args[0]
  4.0 12.1 %halo.1 = (f32[3,320,384]{2,1,0:T(8,128)S(1)}, f32[288,128]{1,0:T(8,128)S(1)}) custom-call(f32[3,256,320]{2,1,0:T(8,128)S(1)} %bitcast.5, f32[256,33]{1,0:T(8,128)S(1)} %copy.8.t_ref), custom_call_target="tpu_custom_call" | custom-call | tf_op jit(solution)/shard_map/halo/pallas_call | solution.py:259
  16.2 0.0 copy-done.2
  16.2 0.0 copy-done.1
  16.2 15.1 %stress.1 = (f32[6,256,320]{2,1,0:T(8,128)S(1)}, f32[6,256,320]{2,1,0:T(8,128)S(1)}) custom-call(f32[3,320,384]{2,1,0:T(8,128)S(1)} %get-tuple-element.6.ext_ref, f32[288,128]{1,0:T(8,128)S(1)} %get-tuple-element.7.text_ref, f32[1,33]{1,0:T(1,128)S(1)} %bitcast.8, f32[1,33]{1,0:T(1,128)S(1)} %bitcast.9, f32[256,33]{1,0:T(8,128)S(1)} %copy.9.ty_ref), custom_call_target="tpu_custom_call" | custom-call | tf_op jit(solution)/shard_map/stress/pallas_call | solution.py:286
  31.3 0.0 copy-start
  31.3 1.4 %copy-done = f32[6,256,320]{2,1,0:T(8,128)} copy-done((f32[6,256,320]{2,1,0:T(8,128)}, f32[6,256,320]{2,1,0:T(8,128)S(1)}, u32[]{:S(2)}) %copy-start) | copy-done | bytes 1966104
  32.7 2.9 %copy.10 = f32[6,1,256,320]{2,3,1,0:T(8,128)} copy(f32[6,1,256,320]{3,2,0,1:T(8,128)} %bitcast.7) | data formatting | bytes 3932160
  35.6 1.8 %copy.11 = f32[6,1,256,320]{2,3,1,0:T(8,128)} copy(f32[6,1,256,320]{3,2,0,1:T(8,128)S(1)} %bitcast.6) | data formatting | bytes 3932160
Async XLA Ops:
  0.6 15.5 %copy-start.2 = (f32[33]{0:T(128)S(1)}, f32[33]{0:T(128)}, u32[]{:S(2)}) copy-start(f32[33]{0:T(128)} %param.8) | copy-start | bytes 400
  0.6 15.5 %copy-start.1 = (f32[33]{0:T(128)S(1)}, f32[33]{0:T(128)}, u32[]{:S(2)}) copy-start(f32[33]{0:T(128)} %param.6) | copy-start | bytes 400
  31.3 1.4 %copy-start = (f32[6,256,320]{2,1,0:T(8,128)}, f32[6,256,320]{2,1,0:T(8,128)S(1)}, u32[]{:S(2)}) copy-start(f32[6,256,320]{2,1,0:T(8,128)S(1)} %get-tuple-element.8) | copy-start | bytes 5898244
where the time goes:
time: 37.8 us; the launch traced here: 37.5 us
  Pallas kernels  27.2 us (72%)
  local copies, waits for them, and re-layouts  9.54 us (25%)
  between operations  0.7 us (2%)
    pallas_call x1, Pallas kernels, local(): pl.pallas_call(functools.partial(stress_kernel, ny, taps), out_shape=(out...  15.1 us
    pallas_call x1, Pallas kernels, local(): pl.pallas_call(functools.partial(halo_kernel, nx, ny, width), out_shape=(...  12.1 us
    unnamed x11, local copies, waits for them, and re-layouts  9.54 us

commit v1 on v0

v1 whole, which is shorter than its diff:
```python
import functools

import jax
import jax.numpy as jnp
from jax import lax
from jax.experimental import pallas as pl
from jax.experimental.pallas import tpu as pltpu
from jax.sharding import PartitionSpec as P

MESH = pl.DeviceIdType.MESH
LANES = 128
SUB = 8
DIRECTIONS = [(1, 0), (-1, 0), (0, 1), (0, -1), (1, 1), (-1, 1), (1, -1), (-1, -1)]
BF = jnp.bfloat16
F32 = jnp.float32


def round_up(value, unit):
    return (value + unit - 1) // unit * unit


def halo_kernel(nx, ny, width, v_ref, t_ref, ext_ref, text_ref,
                pack_d, pack_u, from_d, from_u, from_l, from_r, corners, t_low, t_high,
                send_sem, recv_sem):
    comps, rows, cols = v_ref.shape
    taps = t_ref.shape[0]
    margin = width // 2
    me_x, me_y = lax.axis_index("gx"), lax.axis_index("gy")

    def device(dx, dy):
        return {"gx": lax.rem(me_x + dx + nx, nx), "gy": lax.rem(me_y + dy + ny, ny)}

    barrier = pltpu.get_barrier_semaphore()
    for dx, dy in DIRECTIONS:
        pl.semaphore_signal(barrier, inc=1, device_id=device(dx, dy), device_id_type=MESH)

    per = LANES // width
    groups = rows // width
    for c in range(comps):
        for g in range(groups):
            for q in range(per):
                src = pl.ds(g * width + q * SUB, SUB)
                dst = pl.ds(g * SUB, SUB)
                pack_u[c, dst, q * width:(q + 1) * width] = v_ref[c, src, cols - width:cols]
                pack_d[c, dst, q * width:(q + 1) * width] = v_ref[c, src, 0:width]
    pl.semaphore_wait(barrier, len(DIRECTIONS))

    first, last = pl.ds(0, SUB), pl.ds((groups - 1) * SUB, SUB)
    sources = [
        v_ref.at[:, pl.ds(rows - width, width), :], v_ref.at[:, pl.ds(0, width), :],
        pack_u, pack_d,
        pack_u.at[:, last, :], pack_u.at[:, first, :], pack_d.at[:, last, :], pack_d.at[:, first, :],
    ]
    targets = [from_l, from_r, from_d, from_u] + [corners.at[i] for i in range(4)]
    copies = []
    for i, (dx, dy) in enumerate(DIRECTIONS):
        copies.append((dy, pltpu.make_async_remote_copy(
            src_ref=sources[i], dst_ref=targets[i], send_sem=send_sem.at[i],
            recv_sem=recv_sem.at[i], device_id=device(dx, dy), device_id_type=MESH)))
    for i, (dy, src, dst) in enumerate([
        (1, t_ref.at[:, pl.ds(cols - LANES, LANES)], t_low),
        (-1, t_ref.at[:, pl.ds(0, LANES)], t_high),
    ]):
        n = len(DIRECTIONS) + i
        copies.append((dy, pltpu.make_async_remote_copy(
            src_ref=src, dst_ref=dst, send_sem=send_sem.at[n],
            recv_sem=recv_sem.at[n], device_id=device(0, dy), device_id_type=MESH)))

    has_up, has_down = me_y < ny - 1, me_y > 0
    for dy, copy in copies:
        if dy == 0:
            copy.start()
    for sign, present in ((1, has_up), (-1, has_down)):
        @pl.when(present)
        def _(sign=sign):
            for dy, copy in copies:
                if dy == sign:
                    copy.start()

    rows_ext = rows + 2 * width
    ext_ref[:, :, cols:] = jnp.zeros((comps, rows_ext, LANES), F32)
    text_ref[...] = jnp.zeros_like(text_ref)
    for c in range(comps):
        ext_ref[c, pl.ds(width, rows), 0:cols] = v_ref[c]
    text_ref[0:taps, 0:cols] = t_ref[...]

    def unpack(buf, c, row, lane, count):
        for g in range(count):
            for q in range(per):
                ext_ref[c, pl.ds(row + g * width + q * SUB, SUB), lane:lane + width] = (
                    buf[c, pl.ds(g * SUB, SUB), q * width:(q + 1) * width])

    for sign, present, lane, mid, pair, tile, at in (
        (1, has_down, cols + LANES - width, from_d, (0, 1), t_low, LANES - margin),
        (-1, has_up, cols, from_u, (2, 3), t_high, 0),
    ):
        @pl.when(present)
        def _(sign=sign, lane=lane, mid=mid, pair=pair, tile=tile, at=at):
            for dy, copy in copies:
                if dy == sign:
                    copy.wait_recv()
            for c in range(comps):
                unpack(mid, c, width, lane, groups)
                unpack(corners.at[pair[0]], c, 0, lane, 1)
                unpack(corners.at[pair[1]], c, width + rows, lane, 1)
            text_ref[0:taps, cols + at:cols + at + margin] = tile[:, at:at + margin]

    copies[0][1].wait_recv()
    for c in range(comps):
        ext_ref[c, pl.ds(0, width), 0:cols] = from_l[c]
    copies[1][1].wait_recv()
    for c in range(comps):
        ext_ref[c, pl.ds(width + rows, width), 0:cols] = from_r[c]

    for dy, copy in copies:
        if dy == 0:
            copy.wait_send()
    for sign, present in ((1, has_up), (-1, has_down)):
        @pl.when(present)
        def _(sign=sign):
            for dy, copy in copies:
                if dy == sign:
                    copy.wait_send()


def split(value):
    high = value.astype(BF)
    return high, (value - high.astype(F32)).astype(BF)


def pair_of(p):
    first = jnp.where(p < 3, 0, jnp.where(p < 5, 1, 2))
    second = jnp.where(p < 3, p, jnp.where(p < 5, p - 2, 2))
    return first, second


def dot(a, b):
    return jnp.dot(a, b, preferred_element_type=F32)


def x_weights(w_ref, step, out):
    taps = w_ref.shape[1]
    w = jnp.concatenate([w_ref[...], jnp.zeros((1, LANES - taps), F32)], axis=1)
    w = w / jnp.sum(w)
    band = pltpu.roll(jnp.broadcast_to(w, (LANES, LANES)), 0, 1, stride=1, stride_axis=0)
    high, low = split(band[0:step])
    out[0:step, 0:LANES] = high
    out[0:step, LANES:] = high
    out[step:, 0:LANES] = low
    out[step:, LANES:] = jnp.zeros((step, LANES), BF)


def y_weights(table, taps, first_row, total, cols, main, rest, edge=None):
    margin = (taps - 1) // 2
    lanes = table.shape[1]
    wide = cols + LANES
    k = lax.broadcasted_iota(jnp.int32, (LANES, lanes), 0)
    lane = lax.broadcasted_iota(jnp.int32, (LANES, lanes), 1)
    y = first_row + jnp.where(lane < cols + LANES // 2, lane, lane - wide)
    source = y + k - margin
    keep = (k < taps) & (source >= 0) & (source < total) & (y >= 0) & (y < total)
    w = jnp.where(keep, jnp.concatenate(
        [table, jnp.zeros((LANES - table.shape[0], lanes), F32)], axis=0), 0.0)
    s = jnp.sum(w, axis=0, keepdims=True)
    w = (w / jnp.where(s > 0.0, s, 1.0)).T
    zeros = jnp.zeros((LANES, cols), F32)
    for t in range(lanes // LANES):
        at = slice(t * LANES, (t + 1) * LANES)
        tile = jnp.concatenate([w[at], zeros], axis=1)
        band = pltpu.roll(tile, (t * LANES - margin) % wide, 1, stride=1, stride_axis=0)
        if t * LANES < cols:
            own, halo = band[:, 0:cols].T, band[:, cols:]
            main[0, :, at], main[1, :, at] = split(own)
            high = halo.astype(BF).astype(F32)
            packed = high + pltpu.roll(high, 2 * margin, 1) + pltpu.roll(halo - high, 4 * margin, 1)
            rest[:, at] = packed.T.astype(BF)
        elif edge is not None:
            edge[0], edge[1] = split(band.T)


def y_filter(load, margin, cols, main, rest, put, edge=None):
    value = load()
    high, low = split(value[:, 0:cols])
    halo = value[:, cols:]
    lane = lax.broadcasted_iota(jnp.int32, halo.shape, 1)
    near = jnp.where((lane < margin) | (lane >= LANES - margin), halo, 0.0)
    near_high = near.astype(BF).astype(F32)
    packed = near_high + pltpu.roll(near - near_high, 2 * margin, 1) + pltpu.roll(near_high, 4 * margin, 1)
    z = (dot(high, main[0]) + dot(high, main[1]) + dot(low, main[0])
         + dot(packed.astype(BF), rest[...]))
    put(z, slice(0, cols))
    if edge is not None:
        hh, hl = split(halo)
        z = (dot(high, edge[0, 0:cols]) + dot(high, edge[1, 0:cols]) + dot(low, edge[0, 0:cols])
             + dot(hh, edge[0, cols:]) + dot(hh, edge[1, cols:]) + dot(hl, edge[0, cols:]))
        put(z, slice(cols, cols + LANES))


def x_filter(zh, zl, start, count, lanes, weights, put):
    step = weights.shape[0] // 2
    for s in range(0, count, step):
        size = min(step, count - s)
        at = slice(start + s, start + s + LANES)
        data = jnp.concatenate([zh[at, lanes], zl[at, lanes]], axis=0)
        if size == step:
            r = dot(weights[...], data)
        else:
            r = dot(jnp.concatenate([weights[0:size], weights[step:step + size]], axis=0), data)
        put(s, size, r[0:size] + r[size:])


def stress_kernel(ny, taps, ext_ref, text_ref, gx_ref, tx_ref, ty_ref, sub_ref, ger_ref,
                  coarse, tested, sub, ger, gxw, txw, gym, gyr, gye, tym, tyr, zh, zl, sems):
    comps, rows_ext, wide = ext_ref.shape
    pairs, rows, cols = sub_ref.shape
    margin = (taps - 1) // 2
    rows_mid = rows + 2 * margin
    first_row = lax.axis_index("gy") * cols
    total = cols * ny

    x_weights(gx_ref, gxw.shape[0] // 2, gxw)
    x_weights(tx_ref, txw.shape[0] // 2, txw)
    y_weights(text_ref[...], taps, first_row, total, cols, gym, gyr, gye)
    y_weights(ty_ref[...], taps, first_row, total, cols, tym, tyr)
    zh[pl.ds(rows_ext, LANES), :] = jnp.zeros((LANES, wide), BF)
    zl[pl.ds(rows_ext, LANES), :] = jnp.zeros((LANES, wide), BF)
    own = slice(0, cols)
    everything = slice(0, wide)

    def store(count):
        def put(z, lanes):
            zh[0:count, lanes], zl[0:count, lanes] = split(z)
        return put

    @pl.loop(0, comps)
    def _(c):
        y_filter(lambda: ext_ref[c], margin, cols, gym, gyr, store(rows_ext), gye)

        def put(start, size, value):
            coarse[c, pl.ds(start, size), :] = value

        x_filter(zh, zl, 0, rows_mid, everything, gxw, put)
        y_filter(lambda: coarse[c], margin, cols, tym, tyr, store(rows_mid))

        def put_tested(start, size, value):
            tested[c, pl.ds(start, size), :] = value

        x_filter(zh, zl, 0, rows, own, txw, put_tested)

    def leave(which, source, target, p):
        return pltpu.make_async_copy(source.at[p], target.at[p], sems.at[which, p])

    @pl.loop(0, pairs)
    def _(p):
        i, j = pair_of(p)
        mid = pl.ds(margin, rows_mid)
        y_filter(lambda: ext_ref[i, mid, :] * ext_ref[j, mid, :], margin, cols, gym, gyr,
                 store(rows_mid))

        def put_sub(start, size, value):
            at = pl.ds(margin + start, size)
            sub[p, pl.ds(start, size), :] = value - coarse[i, at, own] * coarse[j, at, own]

        x_filter(zh, zl, 0, rows, own, gxw, put_sub)
        leave(0, sub, sub_ref, p).start()

        y_filter(lambda: coarse[i] * coarse[j], margin, cols, tym, tyr, store(rows_mid))

        def put_ger(start, size, value):
            at = pl.ds(start, size)
            ger[p, at, :] = value - tested[i, at, :] * tested[j, at, :]

        x_filter(zh, zl, 0, rows, own, txw, put_ger)
        leave(1, ger, ger_ref, p).start()

    @pl.loop(0, pairs)
    def _(p):
        leave(0, sub, sub_ref, p).wait()
        leave(1, ger, ger_ref, p).wait()


def local(nx, ny, velocity, grid_x, grid_y, test_x, test_y):
    comps, planes, cols, rows = velocity.shape
    taps = grid_x.shape[0]
    margin = (taps - 1) // 2
    width = 2 * margin
    wide = cols + LANES
    step = LANES - width
    pairs = comps * (comps + 1) // 2
    vmem = pl.BlockSpec(memory_space=pltpu.VMEM)
    anywhere = pl.BlockSpec(memory_space=pl.ANY)
    packed = rows // width * SUB
    subs, gers = [], []
    rows_mid, rows_ext = rows + width, rows + 2 * width
    for plane in range(planes):
        v = jnp.swapaxes(velocity[:, plane], 1, 2)
        ext, text = pl.pallas_call(
            functools.partial(halo_kernel, nx, ny, width),
            out_shape=(
                jax.ShapeDtypeStruct((comps, rows_ext, wide), F32),
                jax.ShapeDtypeStruct((round_up(taps, SUB), wide), F32),
            ),
            in_specs=[vmem] * 2,
            out_specs=(vmem, vmem),
            scratch_shapes=[
                pltpu.VMEM((comps, packed, LANES), F32),
                pltpu.VMEM((comps, packed, LANES), F32),
                pltpu.VMEM((comps, packed, LANES), F32),
                pltpu.VMEM((comps, packed, LANES), F32),
                pltpu.VMEM((comps, width, cols), F32),
                pltpu.VMEM((comps, width, cols), F32),
                pltpu.VMEM((4, comps, SUB, LANES), F32),
                pltpu.VMEM((taps, LANES), F32),
                pltpu.VMEM((taps, LANES), F32),
                pltpu.SemaphoreType.DMA((len(DIRECTIONS) + 2,)),
                pltpu.SemaphoreType.DMA((len(DIRECTIONS) + 2,)),
            ],
            compiler_params=pltpu.CompilerParams(
                collective_id=plane, has_side_effects=True, vmem_limit_bytes=16 << 20),
            name="halo",
        )(v, grid_y.T)
        out = jax.ShapeDtypeStruct((pairs, rows, cols), F32)
        sub, ger = pl.pallas_call(
            functools.partial(stress_kernel, ny, taps),
            out_shape=(out, out),
            in_specs=[vmem] * 5,
            out_specs=(anywhere, anywhere),
            scratch_shapes=[
                pltpu.VMEM((comps, rows_mid, wide), F32),
                pltpu.VMEM((comps, rows, cols), F32),
                pltpu.VMEM((pairs, rows, cols), F32),
                pltpu.VMEM((pairs, rows, cols), F32),
                pltpu.VMEM((2 * step, 2 * LANES), BF),
                pltpu.VMEM((2 * step, 2 * LANES), BF),
                pltpu.VMEM((2, cols, cols), BF),
                pltpu.VMEM((LANES, cols), BF),
                pltpu.VMEM((2, wide, LANES), BF),
                pltpu.VMEM((2, cols, cols), BF),
                pltpu.VMEM((LANES, cols), BF),
                pltpu.VMEM((rows_ext + LANES, wide), BF),
                pltpu.VMEM((rows_ext + LANES, wide), BF),
                pltpu.SemaphoreType.DMA((2, pairs)),
            ],
            compiler_params=pltpu.CompilerParams(vmem_limit_bytes=48 << 20),
            name="stress",
        )(ext, text, grid_x.reshape(1, taps), test_x.reshape(1, taps), test_y.T)
        subs.append(jnp.swapaxes(sub, 1, 2))
        gers.append(jnp.swapaxes(ger, 1, 2))
    return jnp.stack(subs, axis=1), jnp.stack(gers, axis=1)


def solution(mesh):
    nx, ny = mesh.shape["gx"], mesh.shape["gy"]
    field = P(None, None, "gy", "gx")
    return jax.shard_map(
        functools.partial(local, nx, ny),
        mesh=mesh,
        in_specs=(field, P(), P("gy", None), P(), P("gy", None)),
        out_specs=(field, field),
        check_vma=False,
    )
```

time: 37.8 us -> 32 us (0.85)
  local copies, waits for them, and re-layouts: 9.54 us -> 4.06 us
    unnamed x11 -> x10, local copies, waits for them, and re-layouts: 9.54 us -> 4.06 us
where the time goes in v1:
time: 32 us; the launch traced here: 31.7 us
  Pallas kernels  27 us (84%)
  local copies, waits for them, and re-layouts  4.06 us (13%)
  between operations  0.66 us (2%)
    pallas_call x1, Pallas kernels, local(): pl.pallas_call(functools.partial(stress_kernel, ny, taps), out_shape=(out...  15.2 us
    pallas_call x1, Pallas kernels, local(): pl.pallas_call(functools.partial(halo_kernel, nx, ny, width), out_shape=(...  11.8 us
    unnamed x10, local copies, waits for them, and re-layouts  4.06 us

profile of v1, /device:TPU:0, one launch (start us, length us, event | category | flops | bytes accessed | tf_op | source)
XLA Modules:
  0.0 31.7 jit_solution(2340457980605638631)
XLA Ops:
  0.6 0.0 copy-start
  0.6 1.2 %copy-done = f32[3,1,256,320]{2,3,1,0:T(8,128)S(1)} copy-done((f32[3,1,256,320]{2,3,1,0:T(8,128)S(1)}, f32[3,1,256,320]{2,3,1,0:T(8,128)}, u32[]{:S(2)}) %copy-start) | copy-done | bytes 983064
  1.8 0.0 copy-start.1
  1.8 0.8 %copy-done.1 = f32[256,33]{0,1:T(8,128)S(1)} copy-done((f32[256,33]{0,1:T(8,128)S(1)}, f32[256,33]{0,1:T(8,128)}, u32[]{:S(2)}) %copy-start.1) | copy-done | bytes 33816
  2.6 11.8 %halo.1 = (f32[3,384,384]{2,1,0:T(8,128)S(1)}, f32[40,384]{1,0:T(8,128)S(1)}) custom-call(f32[3,320,256]{2,1,0:T(8,128)S(1)} %bitcast.17, f32[33,256]{1,0:T(8,128)S(1)} %bitcast.18), custom_call_target="tpu_custom_call" | custom-call | tf_op jit(solution)/shard_map/halo/pallas_call | solution.py:297
  14.5 0.0 copy-start.2
  14.5 0.8 %copy-done.2 = f32[256,33]{0,1:T(8,128)S(1)} copy-done((f32[256,33]{0,1:T(8,128)S(1)}, f32[256,33]{0,1:T(8,128)}, u32[]{:S(2)}) %copy-start.2) | copy-done | bytes 33816
  15.2 0.0 copy-start.3
  15.2 0.7 %copy-done.3 = f32[33]{0:T(128)S(1)} copy-done((f32[33]{0:T(128)S(1)}, f32[33]{0:T(128)}, u32[]{:S(2)}) %copy-start.3) | copy-done | bytes 156
  15.9 0.0 copy-start.4
  15.9 0.7 %copy-done.4 = f32[33]{0:T(128)S(1)} copy-done((f32[33]{0:T(128)S(1)}, f32[33]{0:T(128)}, u32[]{:S(2)}) %copy-start.4) | copy-done | bytes 156
  16.5 15.2 %stress.1 = (f32[6,320,256]{2,1,0:T(8,128)}, f32[6,320,256]{2,1,0:T(8,128)}) custom-call(f32[3,384,384]{2,1,0:T(8,128)S(1)} %get-tuple-element.6.ext_ref, f32[40,384]{1,0:T(8,128)S(1)} %get-tuple-element.7.text_ref, f32[1,33]{1,0:T(1,128)S(1)} %bitcast.20, f32[1,33]{1,0:T(1,128)S(1)} %bitcast.21, f32[33,256]{1,0:T(8,128)S(1)} %bitcast.19), custom_call_target="tpu_custom_call" | custom-call | tf_op jit(solution)/shard_map/stress/pallas_call | solution.py:323
Async XLA Ops:
  0.6 1.2 %copy-start = (f32[3,1,256,320]{2,3,1,0:T(8,128)S(1)}, f32[3,1,256,320]{2,3,1,0:T(8,128)}, u32[]{:S(2)}) copy-start(f32[3,1,256,320]{2,3,1,0:T(8,128)} %param.5) | copy-start | bytes 2949124
  1.8 0.8 %copy-start.1 = (f32[256,33]{0,1:T(8,128)S(1)}, f32[256,33]{0,1:T(8,128)}, u32[]{:S(2)}) copy-start(f32[256,33]{0,1:T(8,128)} %param.7) | copy-start | bytes 101380
  14.5 0.8 %copy-start.2 = (f32[256,33]{0,1:T(8,128)S(1)}, f32[256,33]{0,1:T(8,128)}, u32[]{:S(2)}) copy-start(f32[256,33]{0,1:T(8,128)} %param.9) | copy-start | bytes 101380
  15.2 0.7 %copy-start.3 = (f32[33]{0:T(128)S(1)}, f32[33]{0:T(128)}, u32[]{:S(2)}) copy-start(f32[33]{0:T(128)} %param.6) | copy-start | bytes 400
  15.9 0.7 %copy-start.4 = (f32[33]{0:T(128)S(1)}, f32[33]{0:T(128)}, u32[]{:S(2)}) copy-start(f32[33]{0:T(128)} %param.8) | copy-start | bytes 400

commit v2 on v1

v2 whole, which is shorter than its diff:
```python
import functools

import jax
import jax.numpy as jnp
from jax import lax
from jax.experimental import pallas as pl
from jax.experimental.pallas import tpu as pltpu
from jax.sharding import PartitionSpec as P

MESH = pl.DeviceIdType.MESH
LANES = 128
SUB = 8
DIRECTIONS = [(1, 0), (-1, 0), (0, 1), (0, -1), (1, 1), (-1, 1), (1, -1), (-1, -1)]
BF = jnp.bfloat16
F32 = jnp.float32


def round_up(value, unit):
    return (value + unit - 1) // unit * unit


def split(value):
    high = value.astype(BF)
    return high, (value - high.astype(F32)).astype(BF)


def pair_of(p):
    first = jnp.where(p < 3, 0, jnp.where(p < 5, 1, 2))
    second = jnp.where(p < 3, p, jnp.where(p < 5, p - 2, 2))
    return first, second


def dot(a, b):
    return jnp.dot(a, b, preferred_element_type=F32)


def x_weights(w_ref, step, out):
    taps = w_ref.shape[1]
    w = jnp.concatenate([w_ref[...], jnp.zeros((1, LANES - taps), F32)], axis=1)
    w = w / jnp.sum(w)
    band = pltpu.roll(jnp.broadcast_to(w, (LANES, LANES)), 0, 1, stride=1, stride_axis=0)
    high, low = split(band[0:step])
    out[0:step, 0:LANES] = high
    out[0:step, LANES:] = high
    out[step:, 0:LANES] = low
    out[step:, LANES:] = jnp.zeros((step, LANES), BF)


def y_weights(table, taps, first_row, total, cols, main, edge=None, tiles=None):
    margin = (taps - 1) // 2
    lanes = table.shape[1]
    wide = cols + LANES
    k = lax.broadcasted_iota(jnp.int32, (LANES, lanes), 0)
    lane = lax.broadcasted_iota(jnp.int32, (LANES, lanes), 1)
    y = first_row + jnp.where(lane < cols + LANES // 2, lane, lane - wide)
    source = y + k - margin
    keep = (k < taps) & (source >= 0) & (source < total) & (y >= 0) & (y < total)
    w = jnp.where(keep, jnp.concatenate(
        [table, jnp.zeros((LANES - table.shape[0], lanes), F32)], axis=0), 0.0)
    s = jnp.sum(w, axis=0, keepdims=True)
    w = (w / jnp.where(s > 0.0, s, 1.0)).T
    zeros = jnp.zeros((LANES, cols), F32)
    for t in (range(lanes // LANES) if tiles is None else tiles):
        at = slice(t * LANES, (t + 1) * LANES)
        tile = jnp.concatenate([w[at], zeros], axis=1)
        band = pltpu.roll(tile, (t * LANES - margin) % wide, 1, stride=1, stride_axis=0)
        if t * LANES < cols:
            own, halo = band[:, 0:cols].T, band[:, cols:]
            own_high, own_low = split(own)
            main[0:cols, at] = own_high
            main[cols:2 * cols, at] = own_low
            main[2 * cols:3 * cols, at] = own_high
            high = halo.astype(BF).astype(F32)
            packed = high + pltpu.roll(high, 2 * margin, 1) + pltpu.roll(halo - high, 4 * margin, 1)
            main[3 * cols:, at] = packed.T.astype(BF)
        else:
            edge_high, edge_low = split(band.T)
            at = 0
            for lo, hi in ((0, cols), (cols, wide)):
                for part in (edge_high, edge_low, edge_high):
                    edge[at:at + hi - lo] = part[lo:hi]
                    at += hi - lo


def halo_kernel(nx, ny, width, v_hbm, t_hbm, gx_hbm, tx_hbm, ty_hbm,
                ext_ref, gxw, txw, gym, gye, tym,
                v_ref, t_ref, gx_ref, tx_ref, ty_ref, text_ref, load_sem, pack_d, pack_u, from_d, from_u, from_l, from_r, corners, t_low, t_high,
                send_sem, recv_sem):
    comps, rows, cols = v_ref.shape
    taps = t_ref.shape[0]
    margin = width // 2
    me_x, me_y = lax.axis_index("gx"), lax.axis_index("gy")

    def device(dx, dy):
        return {"gx": lax.rem(me_x + dx + nx, nx), "gy": lax.rem(me_y + dy + ny, ny)}

    barrier = pltpu.get_barrier_semaphore()
    for dx, dy in DIRECTIONS:
        pl.semaphore_signal(barrier, inc=1, device_id=device(dx, dy), device_id_type=MESH)

    loads = [pltpu.make_async_copy(src, dst, load_sem.at[i]) for i, (src, dst) in enumerate((
        (v_hbm, v_ref), (t_hbm, t_ref), (gx_hbm, gx_ref), (tx_hbm, tx_ref), (ty_hbm, ty_ref)))]
    for load in loads:
        load.start()
    per = LANES // width
    groups = rows // width
    loads[0].wait()
    for c in range(comps):
        for g in range(groups):
            for q in range(per):
                src = pl.ds(g * width + q * SUB, SUB)
                dst = pl.ds(g * SUB, SUB)
                pack_u[c, dst, q * width:(q + 1) * width] = v_ref[c, src, cols - width:cols]
                pack_d[c, dst, q * width:(q + 1) * width] = v_ref[c, src, 0:width]
    pl.semaphore_wait(barrier, len(DIRECTIONS))

    loads[1].wait()
    first, last = pl.ds(0, SUB), pl.ds((groups - 1) * SUB, SUB)
    sources = [
        v_hbm.at[:, pl.ds(rows - width, width), :], v_hbm.at[:, pl.ds(0, width), :],
        pack_u, pack_d,
        pack_u.at[:, last, :], pack_u.at[:, first, :], pack_d.at[:, last, :], pack_d.at[:, first, :],
    ]
    targets = [from_l, from_r, from_d, from_u] + [corners.at[i] for i in range(4)]
    copies = []
    for i, (dx, dy) in enumerate(DIRECTIONS):
        copies.append((dy, pltpu.make_async_remote_copy(
            src_ref=sources[i], dst_ref=targets[i], send_sem=send_sem.at[i],
            recv_sem=recv_sem.at[i], device_id=device(dx, dy), device_id_type=MESH)))
    for i, (dy, src, dst) in enumerate([
        (1, t_ref.at[:, pl.ds(cols - LANES, LANES)], t_low),
        (-1, t_ref.at[:, pl.ds(0, LANES)], t_high),
    ]):
        n = len(DIRECTIONS) + i
        copies.append((dy, pltpu.make_async_remote_copy(
            src_ref=src, dst_ref=dst, send_sem=send_sem.at[n],
            recv_sem=recv_sem.at[n], device_id=device(0, dy), device_id_type=MESH)))

    has_up, has_down = me_y < ny - 1, me_y > 0
    for dy, copy in copies:
        if dy == 0:
            copy.start()
    for sign, present in ((1, has_up), (-1, has_down)):
        @pl.when(present)
        def _(sign=sign):
            for dy, copy in copies:
                if dy == sign:
                    copy.start()

    rows_ext = rows + 2 * width
    ext_ref[:, :, cols:] = jnp.zeros((comps, rows_ext, LANES), F32)
    text_ref[...] = jnp.zeros_like(text_ref)
    for c in range(comps):
        ext_ref[c, pl.ds(width, rows), 0:cols] = v_ref[c]
    text_ref[0:taps, 0:cols] = t_ref[...]
    for load in loads[2:]:
        load.wait()
    first_row, total = me_y * cols, cols * ny
    x_weights(gx_ref, gxw.shape[0] // 2, gxw)
    x_weights(tx_ref, txw.shape[0] // 2, txw)
    own_tiles = range(cols // LANES)
    y_weights(t_ref[...], taps, first_row, total, cols, gym, tiles=own_tiles)
    y_weights(ty_ref[...], taps, first_row, total, cols, tym, tiles=own_tiles)

    def unpack(buf, c, row, lane, count):
        for g in range(count):
            for q in range(per):
                ext_ref[c, pl.ds(row + g * width + q * SUB, SUB), lane:lane + width] = (
                    buf[c, pl.ds(g * SUB, SUB), q * width:(q + 1) * width])

    for sign, present, lane, mid, pair, tile, at in (
        (1, has_down, cols + LANES - width, from_d, (0, 1), t_low, LANES - margin),
        (-1, has_up, cols, from_u, (2, 3), t_high, 0),
    ):
        @pl.when(present)
        def _(sign=sign, lane=lane, mid=mid, pair=pair, tile=tile, at=at):
            for dy, copy in copies:
                if dy == sign:
                    copy.wait_recv()
            for c in range(comps):
                unpack(mid, c, width, lane, groups)
                unpack(corners.at[pair[0]], c, 0, lane, 1)
                unpack(corners.at[pair[1]], c, width + rows, lane, 1)
            text_ref[0:taps, cols + at:cols + at + margin] = tile[:, at:at + margin]

    y_weights(text_ref[...], taps, first_row, total, cols, gym, gye, tiles=(cols // LANES,))
    copies[0][1].wait_recv()
    for c in range(comps):
        ext_ref[c, pl.ds(0, width), 0:cols] = from_l[c]
    copies[1][1].wait_recv()
    for c in range(comps):
        ext_ref[c, pl.ds(width + rows, width), 0:cols] = from_r[c]

    for dy, copy in copies:
        if dy == 0:
            copy.wait_send()
    for sign, present in ((1, has_up), (-1, has_down)):
        @pl.when(present)
        def _(sign=sign):
            for dy, copy in copies:
                if dy == sign:
                    copy.wait_send()


def y_filter(value, margin, cols, main, put, edge=None):
    high, low = split(value[:, 0:cols])
    halo = value[:, cols:]
    lane = lax.broadcasted_iota(jnp.int32, halo.shape, 1)
    near = jnp.where((lane < margin) | (lane >= LANES - margin), halo, 0.0)
    near_high = near.astype(BF).astype(F32)
    packed = near_high + pltpu.roll(near - near_high, 2 * margin, 1) + pltpu.roll(near_high, 4 * margin, 1)
    put(dot(jnp.concatenate([high, high, low, packed.astype(BF)], axis=1), main[...]), slice(0, cols))
    if edge is not None:
        hh, hl = split(halo)
        put(dot(jnp.concatenate([high, high, low, hh, hh, hl], axis=1), edge[...]),
            slice(cols, cols + LANES))


def x_filter(zh, zl, start, count, lanes, weights, put):
    step = weights.shape[0] // 2
    for s in range(0, count, step):
        size = min(step, count - s)
        at = slice(start + s, start + s + LANES)
        data = jnp.concatenate([zh[at, lanes], zl[at, lanes]], axis=0)
        if size == step:
            r = dot(weights[...], data)
        else:
            r = dot(jnp.concatenate([weights[0:size], weights[step:step + size]], axis=0), data)
        put(s, size, r[0:size] + r[size:])


def stress_kernel(margin, batch, ext_ref, gxw, txw, gym, gye, tym, sub_ref, ger_ref,
                  coarse, tested, sub, ger, zh, zl, sems):
    comps, rows_ext, wide = ext_ref.shape
    pairs, rows, cols = sub_ref.shape
    rows_mid = rows + 2 * margin
    own = slice(0, cols)
    everything = slice(0, wide)
    for slot in range(zh.shape[0]):
        zh[slot, pl.ds(rows_ext, LANES), :] = jnp.zeros((LANES, wide), BF)
        zl[slot, pl.ds(rows_ext, LANES), :] = jnp.zeros((LANES, wide), BF)

    def store(slot, n, count):
        def put(z, lanes):
            high, low = split(z)
            for b in range(n):
                at = slice(b * count, (b + 1) * count)
                zh[slot + b, 0:count, lanes], zl[slot + b, 0:count, lanes] = high[at], low[at]
        return put

    def stacked(values):
        return jnp.concatenate(values, axis=0)

    y_filter(stacked([ext_ref[c] for c in range(comps)]), margin, cols, gym,
             store(0, comps, rows_ext), gye)
    for c in range(comps):
        def put(start, size, value, c=c):
            coarse[c, pl.ds(start, size), :] = value

        x_filter(zh.at[c], zl.at[c], 0, rows_mid, everything, gxw, put)
    y_filter(stacked([coarse[c] for c in range(comps)]), margin, cols, tym,
             store(0, comps, rows_mid))
    for c in range(comps):
        def put_tested(start, size, value, c=c):
            tested[c, pl.ds(start, size), :] = value

        x_filter(zh.at[c], zl.at[c], 0, rows, own, txw, put_tested)

    def leave(which, source, target, p):
        return pltpu.make_async_copy(source.at[p], target.at[p], sems.at[which, p])

    mid = pl.ds(margin, rows_mid)

    @pl.loop(0, pairs // batch)
    def _(step):
        indices = [(step * batch + b,) + pair_of(step * batch + b) for b in range(batch)]
        y_filter(stacked([ext_ref[i, mid, :] * ext_ref[j, mid, :] for _, i, j in indices]),
                 margin, cols, gym, store(0, batch, rows_mid))
        y_filter(stacked([coarse[i] * coarse[j] for _, i, j in indices]),
                 margin, cols, tym, store(batch, batch, rows_mid))
        for b, (p, i, j) in enumerate(indices):
            def put_sub(start, size, value, p=p, i=i, j=j):
                at = pl.ds(margin + start, size)
                sub[p, pl.ds(start, size), :] = value - coarse[i, at, own] * coarse[j, at, own]

            x_filter(zh.at[b], zl.at[b], 0, rows, own, gxw, put_sub)
        for b, (p, i, j) in enumerate(indices):
            def put_ger(start, size, value, p=p, i=i, j=j):
                at = pl.ds(start, size)
                ger[p, at, :] = value - tested[i, at, :] * tested[j, at, :]

            x_filter(zh.at[batch + b], zl.at[batch + b], 0, rows, own, txw, put_ger)
        for p, _, _ in indices:
            leave(0, sub, sub_ref, p).start()
            leave(1, ger, ger_ref, p).start()

    @pl.loop(0, pairs)
    def _(p):
        leave(0, sub, sub_ref, p).wait()
        leave(1, ger, ger_ref, p).wait()


def local(nx, ny, velocity, grid_x, grid_y, test_x, test_y):
    comps, planes, cols, rows = velocity.shape
    taps = grid_x.shape[0]
    margin = (taps - 1) // 2
    width = 2 * margin
    wide = cols + LANES
    step = LANES - width
    pairs = comps * (comps + 1) // 2
    batch = 2
    slots = max(comps, 2 * batch)
    vmem = pl.BlockSpec(memory_space=pltpu.VMEM)
    anywhere = pl.BlockSpec(memory_space=pl.ANY)
    packed = rows // width * SUB
    subs, gers = [], []
    rows_mid, rows_ext = rows + width, rows + 2 * width
    for plane in range(planes):
        v = jnp.swapaxes(velocity[:, plane], 1, 2)
        ext, *weights = pl.pallas_call(
            functools.partial(halo_kernel, nx, ny, width),
            out_shape=(
                jax.ShapeDtypeStruct((comps, rows_ext, wide), F32),
                jax.ShapeDtypeStruct((2 * step, 2 * LANES), BF),
                jax.ShapeDtypeStruct((2 * step, 2 * LANES), BF),
                jax.ShapeDtypeStruct((3 * cols + LANES, cols), BF),
                jax.ShapeDtypeStruct((3 * wide, LANES), BF),
                jax.ShapeDtypeStruct((3 * cols + LANES, cols), BF),
            ),
            in_specs=[pl.BlockSpec(memory_space=pltpu.HBM)] * 5,
            out_specs=(vmem,) * 6,
            scratch_shapes=[
                pltpu.VMEM((comps, rows, cols), F32),
                pltpu.VMEM((taps, cols), F32),
                pltpu.VMEM((1, taps), F32),
                pltpu.VMEM((1, taps), F32),
                pltpu.VMEM((taps, cols), F32),
                pltpu.VMEM((round_up(taps, SUB), wide), F32),
                pltpu.SemaphoreType.DMA((5,)),
                pltpu.VMEM((comps, packed, LANES), F32),
                pltpu.VMEM((comps, packed, LANES), F32),
                pltpu.VMEM((comps, packed, LANES), F32),
                pltpu.VMEM((comps, packed, LANES), F32),
                pltpu.VMEM((comps, width, cols), F32),
                pltpu.VMEM((comps, width, cols), F32),
                pltpu.VMEM((4, comps, SUB, LANES), F32),
                pltpu.VMEM((taps, LANES), F32),
                pltpu.VMEM((taps, LANES), F32),
                pltpu.SemaphoreType.DMA((len(DIRECTIONS) + 2,)),
                pltpu.SemaphoreType.DMA((len(DIRECTIONS) + 2,)),
            ],
            compiler_params=pltpu.CompilerParams(
                collective_id=plane, has_side_effects=True, vmem_limit_bytes=48 << 20),
            name="halo",
        )(*[pltpu.with_memory_space_constraint(x, pltpu.HBM) for x in (
            v, grid_y.T, grid_x.reshape(1, taps), test_x.reshape(1, taps), test_y.T)])
        out = jax.ShapeDtypeStruct((pairs, rows, cols), F32)
        sub, ger = pl.pallas_call(
            functools.partial(stress_kernel, margin, batch),
            out_shape=(out, out),
            in_specs=[vmem] * 6,
            out_specs=(anywhere, anywhere),
            scratch_shapes=[
                pltpu.VMEM((comps, rows_mid, wide), F32),
                pltpu.VMEM((comps, rows, cols), F32),
                pltpu.VMEM((pairs, rows, cols), F32),
                pltpu.VMEM((pairs, rows, cols), F32),
                pltpu.VMEM((slots, rows_ext + LANES, wide), BF),
                pltpu.VMEM((slots, rows_ext + LANES, wide), BF),
                pltpu.SemaphoreType.DMA((2, pairs)),
            ],
            compiler_params=pltpu.CompilerParams(vmem_limit_bytes=48 << 20),
            name="stress",
        )(ext, *weights)
        subs.append(jnp.swapaxes(sub, 1, 2))
        gers.append(jnp.swapaxes(ger, 1, 2))
    return jnp.stack(subs, axis=1), jnp.stack(gers, axis=1)


def solution(mesh):
    nx, ny = mesh.shape["gx"], mesh.shape["gy"]
    field = P(None, None, "gy", "gx")
    return jax.shard_map(
        functools.partial(local, nx, ny),
        mesh=mesh,
        in_specs=(field, P(), P("gy", None), P(), P("gy", None)),
        out_specs=(field, field),
        check_vma=False,
    )
```

time: 32 us -> 22 us (0.69)
  Pallas kernels: 27 us -> 21.2 us
  local copies, waits for them, and re-layouts: 4.06 us -> 0 us
    pallas_call x1, Pallas kernels: 15.2 us -> 8.74 us  [local(): pl.pallas_call(functools.partial(stress_kernel, margin, batch), out_shape...]
    unnamed x10 -> x0, local copies, waits for them, and re-layouts: 4.06 us -> none
    pallas_call x1, Pallas kernels: 11.8 us -> 12.5 us  [local(): pl.pallas_call(functools.partial(halo_kernel, nx, ny, width), out_shape=(...]
where the time goes in v2:
time: 22 us; the launch traced here: 21.9 us
  Pallas kernels  21.2 us (96%)
  between operations  0.64 us (3%)
    pallas_call x1, Pallas kernels, local(): pl.pallas_call(functools.partial(halo_kernel, nx, ny, width), out_shape=(...  12.5 us
    pallas_call x1, Pallas kernels, local(): pl.pallas_call(functools.partial(stress_kernel, margin, batch), out_shape...  8.74 us

profile of v2, /device:TPU:0, one launch (start us, length us, event | category | flops | bytes accessed | tf_op | source)
XLA Modules:
  0.0 21.9 jit_solution(3440858399326031281)
XLA Ops:
  0.6 12.5 %halo.1 = (f32[3,384,384]{2,1,0:T(8,128)S(1)}, bf16[192,256]{1,0:T(8,128)(2,1)S(1)}, bf16[192,256]{1,0:T(8,128)(2,1)S(1)}, bf16[896,256]{1,0:T(8,128)(2,1)S(1)},...) custom-call(f32[3,320,256]{2,1,0:T(8,128)} %bitcast.17, f32[33,256]{1,0:T(8,128)} %bitcast.18, ...), custom_call_target="tpu_custom_call" | custom-call | tf_op jit(solution)/shard_map/halo/pallas_call | solution.py:320
  13.1 8.7 %stress.1 = (f32[6,320,256]{2,1,0:T(8,128)}, f32[6,320,256]{2,1,0:T(8,128)}) custom-call(f32[3,384,384]{2,1,0:T(8,128)S(1)} %get-tuple-element.10.ext_ref, bf16[192,256]{1,0:T(8,128)(2,1)S(1)} %get-tuple-element.11.gxw, bf16[192,256]{1,0:T(8,128)(2,1)S(1)} %get-tuple-element.12.txw, bf16[896,256]{1,0:T(8,128)(2,1)S(1)} %get-tuple-element.13.gym, ...), custom_call_target="tpu_custom_call" | custom-call | tf_op jit(solution)/shard_map/stress/pallas_call | solution.py:358

commit v3 on v2

--- a/solution.py
+++ b/solution.py
@@ -104,6 +104,13 @@
         load.start()
     per = LANES // width
     groups = rows // width
+    pl.semaphore_wait(barrier, len(DIRECTIONS))
+    along = [pltpu.make_async_remote_copy(
+        src_ref=v_hbm.at[:, pl.ds(start, width), :], dst_ref=dst, send_sem=send_sem.at[i],
+        recv_sem=recv_sem.at[i], device_id=device(dx, 0), device_id_type=MESH)
+        for i, (dx, start, dst) in enumerate(((1, rows - width, from_l), (-1, 0, from_r)))]
+    for copy in along:
+        copy.start()
     loads[0].wait()
     for c in range(comps):
         for g in range(groups):
@@ -112,20 +119,19 @@
                 dst = pl.ds(g * SUB, SUB)
                 pack_u[c, dst, q * width:(q + 1) * width] = v_ref[c, src, cols - width:cols]
                 pack_d[c, dst, q * width:(q + 1) * width] = v_ref[c, src, 0:width]
-    pl.semaphore_wait(barrier, len(DIRECTIONS))
-
     loads[1].wait()
     first, last = pl.ds(0, SUB), pl.ds((groups - 1) * SUB, SUB)
     sources = [
-        v_hbm.at[:, pl.ds(rows - width, width), :], v_hbm.at[:, pl.ds(0, width), :],
         pack_u, pack_d,
         pack_u.at[:, last, :], pack_u.at[:, first, :], pack_d.at[:, last, :], pack_d.at[:, first, :],
     ]
-    targets = [from_l, from_r, from_d, from_u] + [corners.at[i] for i in range(4)]
-    copies = []
+    targets = [from_d, from_u] + [corners.at[i] for i in range(4)]
+    copies = [(0, copy) for copy in along]
     for i, (dx, dy) in enumerate(DIRECTIONS):
+        if dy == 0:
+            continue
         copies.append((dy, pltpu.make_async_remote_copy(
-            src_ref=sources[i], dst_ref=targets[i], send_sem=send_sem.at[i],
+            src_ref=sources[i - 2], dst_ref=targets[i - 2], send_sem=send_sem.at[i],
             recv_sem=recv_sem.at[i], device_id=device(dx, dy), device_id_type=MESH)))
     for i, (dy, src, dst) in enumerate([
         (1, t_ref.at[:, pl.ds(cols - LANES, LANES)], t_low),
@@ -137,9 +143,6 @@
             recv_sem=recv_sem.at[n], device_id=device(0, dy), device_id_type=MESH)))
 
     has_up, has_down = me_y < ny - 1, me_y > 0
-    for dy, copy in copies:
-        if dy == 0:
-            copy.start()
     for sign, present in ((1, has_up), (-1, has_down)):
         @pl.when(present)
         def _(sign=sign):

time: 22 us -> 22 us (level)
  no operation moved by 1% of the time
where the time goes in v3:
time: 22 us; the launch traced here: 21.9 us
  Pallas kernels  21.2 us (96%)
  between operations  0.64 us (3%)
    pallas_call x1, Pallas kernels, local(): pl.pallas_call(functools.partial(halo_kernel, nx, ny, width), out_shape=(...  12.5 us
    pallas_call x1, Pallas kernels, local(): pl.pallas_call(functools.partial(stress_kernel, margin, batch), out_shape...  8.74 us

profile of v3, /device:TPU:0, one launch (start us, length us, event | category | flops | bytes accessed | tf_op | source)
XLA Modules:
  0.0 21.9 jit_solution(9183195802167044057)
XLA Ops:
  0.6 12.5 %halo.1 = (f32[3,384,384]{2,1,0:T(8,128)S(1)}, bf16[192,256]{1,0:T(8,128)(2,1)S(1)}, bf16[192,256]{1,0:T(8,128)(2,1)S(1)}, bf16[896,256]{1,0:T(8,128)(2,1)S(1)},...) custom-call(f32[3,320,256]{2,1,0:T(8,128)} %bitcast.17, f32[33,256]{1,0:T(8,128)} %bitcast.18, ...), custom_call_target="tpu_custom_call" | custom-call | tf_op jit(solution)/shard_map/halo/pallas_call | solution.py:323
  13.1 8.7 %stress.1 = (f32[6,320,256]{2,1,0:T(8,128)}, f32[6,320,256]{2,1,0:T(8,128)}) custom-call(f32[3,384,384]{2,1,0:T(8,128)S(1)} %get-tuple-element.10.ext_ref, bf16[192,256]{1,0:T(8,128)(2,1)S(1)} %get-tuple-element.11.gxw, bf16[192,256]{1,0:T(8,128)(2,1)S(1)} %get-tuple-element.12.txw, bf16[896,256]{1,0:T(8,128)(2,1)S(1)} %get-tuple-element.13.gym, ...), custom_call_target="tpu_custom_call" | custom-call | tf_op jit(solution)/shard_map/stress/pallas_call | solution.py:361

commit v4 on v3

--- a/solution.py
+++ b/solution.py
@@ -82,9 +82,23 @@
                     at += hi - lo
 
 
+def y_filter(value, margin, cols, main, put, edge=None):
+    high, low = split(value[:, 0:cols])
+    halo = value[:, cols:]
+    lane = lax.broadcasted_iota(jnp.int32, halo.shape, 1)
+    near = jnp.where((lane < margin) | (lane >= LANES - margin), halo, 0.0)
+    near_high = near.astype(BF).astype(F32)
+    packed = near_high + pltpu.roll(near - near_high, 2 * margin, 1) + pltpu.roll(near_high, 4 * margin, 1)
+    put(dot(jnp.concatenate([high, high, low, packed.astype(BF)], axis=1), main[...]), slice(0, cols))
+    if edge is not None:
+        hh, hl = split(halo)
+        put(dot(jnp.concatenate([high, high, low, hh, hh, hl], axis=1), edge[...]),
+            slice(cols, cols + LANES))
+
+
 def halo_kernel(nx, ny, width, v_hbm, t_hbm, gx_hbm, tx_hbm, ty_hbm,
-                ext_ref, gxw, txw, gym, gye, tym,
-                v_ref, t_ref, gx_ref, tx_ref, ty_ref, text_ref, load_sem, pack_d, pack_u, from_d, from_u, from_l, from_r, corners, t_low, t_high,
+                zch, zcl, zph, zpl, gxw, txw, tym,
+                ext_ref, gym, gye, v_ref, t_ref, gx_ref, tx_ref, ty_ref, text_ref, load_sem, pack_d, pack_u, from_d, from_u, from_l, from_r, corners, t_low, t_high,
                 send_sem, recv_sem):
     comps, rows, cols = v_ref.shape
     taps = t_ref.shape[0]
@@ -187,12 +201,44 @@
             text_ref[0:taps, cols + at:cols + at + margin] = tile[:, at:at + margin]
 
     y_weights(text_ref[...], taps, first_row, total, cols, gym, gye, tiles=(cols // LANES,))
+
+    def store(high_ref, low_ref, places, count):
+        def put(z, lanes):
+            high, low = split(z)
+            for n, (slot, row) in enumerate(places):
+                at = slice(n * count, (n + 1) * count)
+                high_ref[slot, pl.ds(row, count), lanes] = high[at]
+                low_ref[slot, pl.ds(row, count), lanes] = low[at]
+        return put
+
+    def stacked(values):
+        return jnp.concatenate(values, axis=0)
+
+    combos = [(i, j) for i in range(comps) for j in range(i, comps)]
+    for ref, tail in ((zch, rows_ext), (zcl, rows_ext), (zph, rows_ext - width), (zpl, rows_ext - width)):
+        ref[:, pl.ds(tail, LANES), :] = jnp.zeros((ref.shape[0], LANES, ref.shape[2]), BF)
+    body = pl.ds(width, rows)
+    y_filter(stacked([ext_ref[c, body, :] for c in range(comps)]), margin, cols, gym,
+             store(zch, zcl, [(c, width) for c in range(comps)], rows), gye)
+    for start in range(0, len(combos), 2):
+        some = list(enumerate(combos))[start:start + 2]
+        y_filter(stacked([ext_ref[i, body, :] * ext_ref[j, body, :] for _, (i, j) in some]), margin,
+                 cols, gym, store(zph, zpl, [(p, margin) for p, _ in some], rows))
+
     copies[0][1].wait_recv()
     for c in range(comps):
         ext_ref[c, pl.ds(0, width), 0:cols] = from_l[c]
     copies[1][1].wait_recv()
     for c in range(comps):
         ext_ref[c, pl.ds(width + rows, width), 0:cols] = from_r[c]
+    ends = [(0, 0), (width + rows, width + rows)]
+    y_filter(stacked([ext_ref[c, pl.ds(at, width), :] for c in range(comps) for at, _ in ends]),
+             margin, cols, gym,
+             store(zch, zcl, [(c, to) for c in range(comps) for _, to in ends], width), gye)
+    ends = [(margin, 0), (width + rows, margin + rows)]
+    y_filter(stacked([ext_ref[i, pl.ds(at, margin), :] * ext_ref[j, pl.ds(at, margin), :]
+                      for i, j in combos for at, _ in ends]), margin, cols, gym,
+             store(zph, zpl, [(p, to) for p in range(len(combos)) for _, to in ends], margin))
 
     for dy, copy in copies:
         if dy == 0:
@@ -203,20 +249,6 @@
             for dy, copy in copies:
                 if dy == sign:
                     copy.wait_send()
-
-
-def y_filter(value, margin, cols, main, put, edge=None):
-    high, low = split(value[:, 0:cols])
-    halo = value[:, cols:]
-    lane = lax.broadcasted_iota(jnp.int32, halo.shape, 1)
-    near = jnp.where((lane < margin) | (lane >= LANES - margin), halo, 0.0)
-    near_high = near.astype(BF).astype(F32)
-    packed = near_high + pltpu.roll(near - near_high, 2 * margin, 1) + pltpu.roll(near_high, 4 * margin, 1)
-    put(dot(jnp.concatenate([high, high, low, packed.astype(BF)], axis=1), main[...]), slice(0, cols))
-    if edge is not None:
-        hh, hl = split(halo)
-        put(dot(jnp.concatenate([high, high, low, hh, hh, hl], axis=1), edge[...]),
-            slice(cols, cols + LANES))
 
 
 def x_filter(zh, zl, start, count, lanes, weights, put):
@@ -232,16 +264,16 @@
         put(s, size, r[0:size] + r[size:])
 
 
-def stress_kernel(margin, batch, ext_ref, gxw, txw, gym, gye, tym, sub_ref, ger_ref,
+def stress_kernel(margin, batch, zch, zcl, zph, zpl, gxw, txw, tym, sub_ref, ger_ref,
                   coarse, tested, sub, ger, zh, zl, sems):
-    comps, rows_ext, wide = ext_ref.shape
+    comps, wide = zch.shape[0], zch.shape[2]
     pairs, rows, cols = sub_ref.shape
     rows_mid = rows + 2 * margin
     own = slice(0, cols)
     everything = slice(0, wide)
     for slot in range(zh.shape[0]):
-        zh[slot, pl.ds(rows_ext, LANES), :] = jnp.zeros((LANES, wide), BF)
-        zl[slot, pl.ds(rows_ext, LANES), :] = jnp.zeros((LANES, wide), BF)
+        zh[slot, pl.ds(rows_mid, LANES), :] = jnp.zeros((LANES, cols), BF)
+        zl[slot, pl.ds(rows_mid, LANES), :] = jnp.zeros((LANES, cols), BF)
 
     def store(slot, n, count):
         def put(z, lanes):
@@ -254,13 +286,11 @@
     def stacked(values):
         return jnp.concatenate(values, axis=0)
 
-    y_filter(stacked([ext_ref[c] for c in range(comps)]), margin, cols, gym,
-             store(0, comps, rows_ext), gye)
     for c in range(comps):
         def put(start, size, value, c=c):
             coarse[c, pl.ds(start, size), :] = value
 
-        x_filter(zh.at[c], zl.at[c], 0, rows_mid, everything, gxw, put)
+        x_filter(zch.at[c], zcl.at[c], 0, rows_mid, everything, gxw, put)
     y_filter(stacked([coarse[c] for c in range(comps)]), margin, cols, tym,
              store(0, comps, rows_mid))
     for c in range(comps):
@@ -271,28 +301,24 @@
 
     def leave(which, source, target, p):
         return pltpu.make_async_copy(source.at[p], target.at[p], sems.at[which, p])
-
-    mid = pl.ds(margin, rows_mid)
 
     @pl.loop(0, pairs // batch)
     def _(step):
         indices = [(step * batch + b,) + pair_of(step * batch + b) for b in range(batch)]
-        y_filter(stacked([ext_ref[i, mid, :] * ext_ref[j, mid, :] for _, i, j in indices]),
-                 margin, cols, gym, store(0, batch, rows_mid))
         y_filter(stacked([coarse[i] * coarse[j] for _, i, j in indices]),
-                 margin, cols, tym, store(batch, batch, rows_mid))
+                 margin, cols, tym, store(0, batch, rows_mid))
         for b, (p, i, j) in enumerate(indices):
             def put_sub(start, size, value, p=p, i=i, j=j):
                 at = pl.ds(margin + start, size)
                 sub[p, pl.ds(start, size), :] = value - coarse[i, at, own] * coarse[j, at, own]
 
-            x_filter(zh.at[b], zl.at[b], 0, rows, own, gxw, put_sub)
+            x_filter(zph.at[p], zpl.at[p], 0, rows, own, gxw, put_sub)
         for b, (p, i, j) in enumerate(indices):
             def put_ger(start, size, value, p=p, i=i, j=j):
                 at = pl.ds(start, size)
                 ger[p, at, :] = value - tested[i, at, :] * tested[j, at, :]
 
-            x_filter(zh.at[batch + b], zl.at[batch + b], 0, rows, own, txw, put_ger)
+            x_filter(zh.at[b], zl.at[b], 0, rows, own, txw, put_ger)
         for p, _, _ in indices:
             leave(0, sub, sub_ref, p).start()
             leave(1, ger, ger_ref, p).start()
@@ -312,7 +338,7 @@
     step = LANES - width
     pairs = comps * (comps + 1) // 2
     batch = 2
-    slots = max(comps, 2 * batch)
+    slots = max(comps, batch)
     vmem = pl.BlockSpec(memory_space=pltpu.VMEM)
     anywhere = pl.BlockSpec(memory_space=pl.ANY)
     packed = rows // width * SUB
@@ -320,19 +346,23 @@
     rows_mid, rows_ext = rows + width, rows + 2 * width
     for plane in range(planes):
         v = jnp.swapaxes(velocity[:, plane], 1, 2)
-        ext, *weights = pl.pallas_call(
+        middle = pl.pallas_call(
             functools.partial(halo_kernel, nx, ny, width),
             out_shape=(
-                jax.ShapeDtypeStruct((comps, rows_ext, wide), F32),
+                jax.ShapeDtypeStruct((comps, rows_ext + LANES, wide), BF),
+                jax.ShapeDtypeStruct((comps, rows_ext + LANES, wide), BF),
+                jax.ShapeDtypeStruct((pairs, rows_mid + LANES, cols), BF),
+                jax.ShapeDtypeStruct((pairs, rows_mid + LANES, cols), BF),
                 jax.ShapeDtypeStruct((2 * step, 2 * LANES), BF),
                 jax.ShapeDtypeStruct((2 * step, 2 * LANES), BF),
                 jax.ShapeDtypeStruct((3 * cols + LANES, cols), BF),
-                jax.ShapeDtypeStruct((3 * wide, LANES), BF),
-                jax.ShapeDtypeStruct((3 * cols + LANES, cols), BF),
             ),
             in_specs=[pl.BlockSpec(memory_space=pltpu.HBM)] * 5,
-            out_specs=(vmem,) * 6,
+            out_specs=(vmem,) * 7,
             scratch_shapes=[
+                pltpu.VMEM((comps, rows_ext, wide), F32),
+                pltpu.VMEM((3 * cols + LANES, cols), BF),
+                pltpu.VMEM((3 * wide, LANES), BF),
                 pltpu.VMEM((comps, rows, cols), F32),
                 pltpu.VMEM((taps, cols), F32),
                 pltpu.VMEM((1, taps), F32),
@@ -353,7 +383,7 @@
                 pltpu.SemaphoreType.DMA((len(DIRECTIONS) + 2,)),
             ],
             compiler_params=pltpu.CompilerParams(
-                collective_id=plane, has_side_effects=True, vmem_limit_bytes=48 << 20),
+                collective_id=plane, has_side_effects=True, vmem_limit_bytes=40 << 20),
             name="halo",
         )(*[pltpu.with_memory_space_constraint(x, pltpu.HBM) for x in (
             v, grid_y.T, grid_x.reshape(1, taps), test_x.reshape(1, taps), test_y.T)])
@@ -361,20 +391,20 @@
         sub, ger = pl.pallas_call(
             functools.partial(stress_kernel, margin, batch),
             out_shape=(out, out),
-            in_specs=[vmem] * 6,
+            in_specs=[vmem] * 7,
             out_specs=(anywhere, anywhere),
             scratch_shapes=[
                 pltpu.VMEM((comps, rows_mid, wide), F32),
                 pltpu.VMEM((comps, rows, cols), F32),
                 pltpu.VMEM((pairs, rows, cols), F32),
                 pltpu.VMEM((pairs, rows, cols), F32),
-                pltpu.VMEM((slots, rows_ext + LANES, wide), BF),
-                pltpu.VMEM((slots, rows_ext + LANES, wide), BF),
+                pltpu.VMEM((slots, rows_mid + LANES, cols), BF),
+                pltpu.VMEM((slots, rows_mid + LANES, cols), BF),
                 pltpu.SemaphoreType.DMA((2, pairs)),
             ],
-            compiler_params=pltpu.CompilerParams(vmem_limit_bytes=48 << 20),
+            compiler_params=pltpu.CompilerParams(vmem_limit_bytes=44 << 20),
             name="stress",
-        )(ext, *weights)
+        )(*middle)
         subs.append(jnp.swapaxes(sub, 1, 2))
         gers.append(jnp.swapaxes(ger, 1, 2))
     return jnp.stack(subs, axis=1), jnp.stack(gers, axis=1)

time: 22 us -> 23.6 us (1.073)
  Pallas kernels: 21.2 us -> 22.8 us
    pallas_call x1, Pallas kernels: 12.5 us -> 15.9 us  [local(): pl.pallas_call(functools.partial(halo_kernel, nx, ny, width), out_shape=(...]
    pallas_call x1, Pallas kernels: 8.74 us -> 6.89 us  [local(): pl.pallas_call(functools.partial(stress_kernel, margin, batch), out_shape...]
where the time goes in v4:
time: 23.6 us; the launch traced here: 23.4 us
  Pallas kernels  22.8 us (97%)
  between operations  0.64 us (3%)
    pallas_call x1, Pallas kernels, local(): pl.pallas_call(functools.partial(halo_kernel, nx, ny, width), out_shape=(...  15.9 us
    pallas_call x1, Pallas kernels, local(): pl.pallas_call(functools.partial(stress_kernel, margin, batch), out_shape...  6.89 us

profile of v4, /device:TPU:0, one launch (start us, length us, event | category | flops | bytes accessed | tf_op | source)
XLA Modules:
  0.0 23.4 jit_solution(280066072258332052)
XLA Ops:
  0.6 15.9 %halo.1 = (bf16[3,512,384]{2,1,0:T(8,128)(2,1)S(1)}, bf16[3,512,384]{2,1,0:T(8,128)(2,1)S(1)}, bf16[6,480,256]{2,1,0:T(8,128)(2,1)S(1)}, bf16[6,480,256]{2,1,0:T...) custom-call(f32[3,320,256]{2,1,0:T(8,128)} %bitcast.17, ...), custom_call_target="tpu_custom_call" | custom-call | tf_op jit(solution)/shard_map/halo/pallas_call | solution.py:349
  16.5 6.9 %stress.1 = (f32[6,320,256]{2,1,0:T(8,128)}, f32[6,320,256]{2,1,0:T(8,128)}) custom-call(bf16[3,512,384]{2,1,0:T(8,128)(2,1)S(1)} %get-tuple-element.11.zch, bf16[3,512,384]{2,1,0:T(8,128)(2,1)S(1)} %get-tuple-element.12.zcl, bf16[6,480,256]{2,1,0:T(8,128)(2,1)S(1)} %get-tuple-element.13.zph, bf16[6,480,256]{2,1,0:T(8,128)(2,1)S(1)} %get-tuple-element.14.zpl, ...), custom_call_target="tpu_custom_call" | custom-call | tf_op jit(solution)/shard_map/stress/pallas_call | solution.py:391
